TPU v7x, 32 devices: a whole 2x2x4 slice. The times are simulated.
32 devices in a mesh: row: 8 (over z, x), col: 2 (over y), rep: 2 (over core).
Axes of the slice: x: 2, y: 2, z: 4, core: 2. Of those that a mesh axis runs over, the one named last changes fastest.
Arguments:
- rhs_low: float32 [2, 3, 8, 256, 128], P('rep', None, 'row', 'col'), may hold values from -6 to 6
- rhs_top: float32 [8, 256, 128], P('row', 'col'), may hold values from -6 to 6
- inv_low: float32 [2, 3, 8, 256, 256], P('rep', None, 'row', 'col'), as said below
- inv_top: float32 [8, 256, 256], P('row', 'col'), as said below
- blocks: float32 [2, 8, 2, 3, 4, 256, 256], P('rep', 'row', 'col'), may hold values from -0.1875 to 0.1875
- slot_map: int32 [2, 8, 2, 3, 4, 2], P('rep', 'row', 'col'), may hold values from 0 to 3, as said below
Outputs:
- sol_low: float32 [2, 3, 8, 256, 128], P('rep', None, 'row', 'col')
- sol_top: float32 [8, 256, 128], P('row', 'col')
Inputs may be any that keep to these rules, and one draw needn't show every extreme that they name: slot_map[s, p, q, l, k] = (t, c): t = 0 marks an empty slot (then c = 0); else 3 >= t > l and c < 4. The live pairs (t, c) of one device and one l are distinct, live slots come before empty ones, every device has at least one live slot for each l, and for each l some device has all 4 slots live. `inv_low`: each block is a dense matrix with a positive diagonal of about one and full off-diagonal entries. `inv_top`: each block is a dense matrix with a positive diagonal of about one and full off-diagonal entries.
All inputs are finite; a program needn't handle non-finite values.
Results may differ from a plain program's by a relative error of at most 0.0003.
Values sent between devices are 32-bit elements; how exact they have to be, the bound alone decides.
A program may use at most 64 MiB of HBM per device.

v0:
```python
import functools
import jax
import jax.numpy as jnp
from jax import lax
from jax.experimental import pallas as pl
from jax.experimental.pallas import tpu as pltpu
from jax.sharding import PartitionSpec as P

MESH = pl.DeviceIdType.MESH


def split(value):
    high = value.astype(jnp.bfloat16)
    low = (value - high.astype(jnp.float32)).astype(jnp.bfloat16)
    return high, low


def dot3(value, right_high, right_low):
    high, low = split(value)
    count = value.shape[0]
    turned = (((1,), (1,)), ((), ()))
    both = jnp.concatenate([high, low], axis=0)
    wide = lax.dot_general(both, right_high, turned, preferred_element_type=jnp.float32)
    rest = lax.dot_general(high, right_low, turned, preferred_element_type=jnp.float32)
    return wide[:count] + (wide[count:] + rest)


def kernel(
    rows, cols, reps, levels, slots, streams,
    rhs_low, rhs_top, inv_low_hbm, inv_top_hbm, blocks_hbm, table_hbm, out_low, out_top,
    table, table_sem, blocks, inverse, right0, rhs, partial, whole, partial_in, top_in, line, inv_high, inv_rest,
    tile_high, tile_rest,
    load_sem, inv_sem, rhs_sem, right_send, right_recv, part_send, part_recv, top_send, top_recv,
    line_send, line_recv, col_send, col_recv, *columns,
):
    row = lax.axis_index("row")
    q = lax.axis_index("col")
    rep = lax.axis_index("rep")
    share = rows // cols
    a = row // cols
    b = row % cols
    part = rhs_top.shape[0]
    depth = partial.shape[2]

    loads = [
        pltpu.make_async_copy(blocks_hbm.at[l], blocks.at[l], load_sem.at[l]) for l in range(levels)
    ]
    inv_loads = [
        pltpu.make_async_copy(inv_low_hbm.at[t] if t < levels else inv_top_hbm, inverse.at[t], inv_sem.at[t])
        for t in range(levels + 1)
    ]
    rhs_loads = [pltpu.make_async_copy(rhs_low.at[0], right0.at[q], rhs_sem.at[0])]
    for t in range(1, levels + 1):
        rhs_loads.append(
            pltpu.make_async_copy(rhs_low.at[t] if t < levels else rhs_top, rhs.at[t], rhs_sem.at[t])
        )
    for load in [rhs_loads[0], inv_loads[0], loads[0]] + rhs_loads[1:] + inv_loads[1:] + loads[1:]:
        load.start()

    table_load = pltpu.make_async_copy(table_hbm, table, table_sem)
    table_load.start()
    col_peers = [lax.rem(q + d, cols) for d in range(1, cols)]
    rep_peers = [lax.rem(rep + d, reps) for d in range(1, reps)]

    barrier = pltpu.get_barrier_semaphore()
    count = 0
    for dr in range(cols):
        for dc in range(cols):
            if dr or dc:
                pl.semaphore_signal(
                    barrier, inc=1, device_id_type=MESH,
                    device_id={"row": a * cols + lax.rem(b + dr, cols), "col": lax.rem(q + dc, cols)},
                )
                count += 1
    for d in range(1, share):
        pl.semaphore_signal(
            barrier, inc=1, device_id_type=MESH,
            device_id={"row": lax.rem(a + d, share) * cols + b},
        )
        count += 1
    for peer in rep_peers:
        pl.semaphore_signal(barrier, inc=1, device_id_type=MESH, device_id={"rep": peer})
        count += 1
    pl.semaphore_wait(barrier, count)

    started = []
    conditional = []

    def send(src, dst, send_sem, recv_sem, device):
        return pltpu.make_async_remote_copy(
            src_ref=src, dst_ref=dst, send_sem=send_sem, recv_sem=recv_sem,
            device_id=device, device_id_type=MESH,
        )

    def go(copy):
        copy.start()
        started.append(copy)

    def begin(d, source, peer):
        return send(rhs_low.at[0], right0.at[source], right_send.at[d], right_recv.at[source], {"col": peer})

    for d, peer in enumerate(col_peers):
        go(begin(d, q, peer))

    def take_inverse(t):
        inv_loads[t].wait()
        high, low = split(inverse[t])
        inv_high[t] = high
        inv_rest[t] = low

    def take_rhs(t):
        rhs_loads[t].wait()
        turned = rhs[t].T
        if t == levels:
            turned = jnp.where(rep == 0, turned, 0.0)
        spaced = jnp.concatenate([jnp.where(q == j, turned, 0.0) for j in range(cols)], axis=1)
        for s in range(streams):
            partial[t, s] = spaced[s * depth:(s + 1) * depth]

    take_inverse(0)
    table_load.wait()

    def order(i, here):
        low_side = jnp.where(i >= here, i + 1, i)
        mirror = share - 1 - here
        high_side = share - 1 - jnp.where(i >= mirror, i + 1, i)
        return jnp.where(2 * here < share, low_side, high_side)

    def hop(t, s, source, d, peer, src):
        return send(
            src.at[t, s], partial_in.at[t, source, s], part_send.at[t, d, s], part_recv.at[t, source, s],
            {"col": peer},
        )

    def exchange(t, s, src):
        for d, peer in enumerate(col_peers):
            go(hop(t, s, q, d, peer, src))

    def collect(t, s, src):
        total = src[t, s]
        for d, peer in enumerate(col_peers):
            hop(t, s, peer, d, peer, src).wait_recv()
            total = total + partial_in[t, peer, s]
        return total

    def lift(s, d, peer):
        return send(partial.at[levels, s], top_in.at[d, s], top_send.at[d, s], top_recv.at[d, s], {"rep": peer})

    def along(l, s, i, source, target):
        return send(
            line.at[l, s, source], line.at[l, s, source], line_send.at[l, s, i], line_recv.at[l, s, source],
            {"row": target * cols + b},
        )

    def spread(l, s, c, index):
        for d in range(cols):
            copy = send(
                line.at[l, s, c], columns[l * streams + s].at[c, q], col_send.at[l, s, index, d],
                col_recv.at[l, s, c, q],
                {"row": a * cols + lax.rem(b + d, cols), "col": b},
            )
            if d == 0:
                pl.when(q != b)(copy.start)
                conditional.append(copy)
            else:
                go(copy)

        @pl.when(q == b)
        def _():
            columns[l * streams + s][c, q] = line[l, s, c]

    residue0 = None
    for l in range(levels):
        pieces = []
        for s in range(streams):
            if l == 0:
                if s == 0:
                    for d, peer in enumerate(col_peers):
                        begin(d, peer, peer).wait_recv()
                    rhs_loads[0].wait()
                    residue0 = right0[...].reshape(part * cols, right0.shape[2]).T
                residue = residue0[s * depth:(s + 1) * depth]
            else:
                residue = collect(l, s, partial)
            solved = dot3(residue, inv_high[l], inv_rest[l])
            line[l, s, a] = solved
            for i in reversed(range(share - 1)):
                go(along(l, s, i, a, order(i, a)))
            spread(l, s, a, share - 1)
            pieces.append(solved)
        loads[l].wait()
        for k in range(slots):
            high, low = split(blocks[l, k])
            tile_high[k] = high
            tile_rest[k] = low
        for s in range(streams):
            for i in range(share - 1):
                c = order(i, a)
                along(l, s, i, c, c).wait_recv()
                spread(l, s, c, i)
        out_low[l] = jnp.concatenate(pieces, axis=0).T
        take_inverse(l + 1)
        if l == 0:
            for t in range(1, levels + 1):
                take_rhs(t)
        later = []

        def add(t, s, products):
            total = partial[t, s]
            for k in range(slots):
                total = total - jnp.where(table[l, 0, k] == t, products[k], 0.0)
            partial[t, s] = total

        for s in range(streams):
            for c in range(share):
                for source in range(cols):
                    copy = send(
                        line.at[l, s, c], columns[l * streams + s].at[c, source], col_send.at[l, s, c, 0],
                        col_recv.at[l, s, c, source],
                        {"row": a * cols + q, "col": lax.rem(q + 1, cols)},
                    )
                    pl.when(jnp.logical_or(b != q, source != q))(copy.wait_recv)
            products = []
            for k in range(slots):
                found = columns[l * streams + s][table[l, 1, k]]
                picked = jnp.concatenate([found[j] for j in range(cols)], axis=1)
                products.append(dot3(picked, tile_high[k], tile_rest[k]))
            later.append((s, products))
            add(l + 1, s, products)
            if l + 1 < levels:
                exchange(l + 1, s, partial)
            if l + 1 == levels:
                for d, peer in enumerate(rep_peers):
                    go(lift(s, d, peer))
        for s, products in later:
            for t in range(l + 2, levels + 1):
                add(t, s, products)

    for s in range(streams):
        total = partial[levels, s]
        for d, peer in enumerate(rep_peers):
            lift(s, d, peer).wait_recv()
            total = total + top_in[d, s]
        whole[levels, s] = total
        exchange(levels, s, whole)
    pieces = []
    for s in range(streams):
        pieces.append(dot3(collect(levels, s, whole), inv_high[levels], inv_rest[levels]))
    out_top[...] = jnp.concatenate(pieces, axis=0).T

    for copy in started:
        copy.wait_send()

    @pl.when(q != b)
    def _():
        for copy in conditional:
            copy.wait_send()


def per_device(rows, cols, reps, rhs_low, rhs_top, inv_low, inv_top, blocks, slot_map):
    rhs_low, rhs_top = rhs_low[0, :, 0], rhs_top[0]
    inv_low, inv_top = inv_low[0, :, 0], inv_top[0]
    blocks, table = blocks[0, 0, 0], jnp.swapaxes(slot_map[0, 0, 0], 1, 2)
    levels, slots, size = blocks.shape[:3]
    rhs_low, rhs_top, inv_low, inv_top, blocks, table = [
        pltpu.with_memory_space_constraint(x, pltpu.HBM) for x in (rhs_low, rhs_top, inv_low, inv_top, blocks, table)
    ]
    part, width = rhs_top.shape
    share = rows // cols
    vmem = pl.BlockSpec(memory_space=pltpu.VMEM)
    hbm = pl.BlockSpec(memory_space=pltpu.HBM)
    streams = 4
    depth = width // streams
    dma = pltpu.SemaphoreType.DMA
    f32, bf16 = jnp.float32, jnp.bfloat16
    sol_low, sol_top = pl.pallas_call(
        functools.partial(kernel, rows, cols, reps, levels, slots, streams),
        out_shape=(
            jax.ShapeDtypeStruct((levels, part, width), f32),
            jax.ShapeDtypeStruct((part, width), f32),
        ),
        in_specs=[hbm, hbm, hbm, hbm, hbm, hbm],
        out_specs=(vmem, vmem),
        scratch_shapes=[
            pltpu.SMEM(table.shape, jnp.int32),
            dma(()),
            pltpu.VMEM((levels, slots, size, size), f32),
            pltpu.VMEM((levels + 1, part, size), f32),
            pltpu.VMEM((cols, part, width), f32),
            pltpu.VMEM((levels + 1, part, width), f32),
            pltpu.VMEM((levels + 1, streams, depth, size), f32),
            pltpu.VMEM((levels + 1, streams, depth, size), f32),
            pltpu.VMEM((levels + 1, cols, streams, depth, size), f32),
            pltpu.VMEM((reps - 1, streams, depth, size), f32),
            pltpu.VMEM((levels, streams, share, depth, part), f32),
            pltpu.VMEM((levels + 1, part, size), bf16),
            pltpu.VMEM((levels + 1, part, size), bf16),
            pltpu.VMEM((slots, size, size), bf16),
            pltpu.VMEM((slots, size, size), bf16),
            dma((levels,)),
            dma((levels + 1,)),
            dma((levels + 1,)),
            dma((cols - 1,)),
            dma((cols,)),
            dma((levels + 1, cols - 1, streams)),
            dma((levels + 1, cols, streams)),
            dma((reps - 1, streams)),
            dma((reps - 1, streams)),
            dma((levels, streams, share - 1)),
            dma((levels, streams, share)),
            dma((levels, streams, share, cols)),
            dma((levels, streams, share, cols)),
        ]
        + [pltpu.VMEM((share, cols, depth, part), f32)] * (levels * streams),
        compiler_params=pltpu.CompilerParams(
            collective_id=0, has_side_effects=True, vmem_limit_bytes=48 * 1024 * 1024
        ),
    )(rhs_low, rhs_top, inv_low, inv_top, blocks, table)
    return (sol_low[None, :, None], sol_top[None])


def solution(mesh):
    in_specs = (
        P("rep", None, "row", "col", None),
        P("row", "col", None),
        P("rep", None, "row", "col", None),
        P("row", "col", None),
        P("rep", "row", "col", None, None, None, None),
        P("rep", "row", "col", None, None, None),
    )
    out_specs = (P("rep", None, "row", "col", None), P("row", "col", None))
    body = functools.partial(per_device, mesh.shape["row"], mesh.shape["col"], mesh.shape["rep"])
    return jax.shard_map(body, mesh=mesh, in_specs=in_specs, out_specs=out_specs, check_vma=False)
```

profile of v0, /device:TPU:0, one launch (start us, length us, event | category | flops | bytes accessed | tf_op | source)
XLA Modules:
  0.0 53.0 jit_solution(2686726041894160039)
XLA Ops:
  0.6 51.1 %shard_map.77 = (f32[3,128,128]{2,1,0:T(8,128)S(1)}, f32[128,128]{1,0:T(8,128)S(1)}) custom-call(f32[3,128,128]{2,1,0:T(8,128)} %bitcast.16, f32[128,128]{1,0:T(8,128)} %bitcast.18, f32[3,128,256]{2,1,0:T(8,128)} %bitcast.15, f32[128,256]{1,0:T(8,128)} %bitcast.17, f32[3,4,256,256]{3,2,1,0:T(8,128)} %bitcast.14, s32[3,2,4]{2,1,0:T(2,128)} %bitcast.19), custom_call_target="tpu_custom_call" | custom-call | tf_op jit(solution)/shard_map/pallas_call | solution.py:276
  51.7 0.7 %copy.11 = f32[1,3,1,128,128]{4,3,2,1,0:T(8,128)} copy(f32[1,3,1,128,128]{4,3,2,1,0:T(8,128)S(1)} %bitcast.12) | data formatting | bytes 393216
  52.4 0.6 %copy.12 = f32[1,128,128]{2,1,0:T(8,128)} copy(f32[1,128,128]{2,1,0:T(8,128)S(1)} %bitcast.13) | data formatting | bytes 131072
where the time goes:
time: 53.2 us; the launch traced here: 53 us
  Pallas kernels  51.1 us (96%)
  local copies, waits for them, and re-layouts  1.31 us (2%)
  between operations  0.64 us (1%)
    pallas_call x1, Pallas kernels, per_device(): pl.pallas_call(functools.partial(kernel, rows, cols, reps, levels, slots,...  51.1 us
    unnamed x2, local copies, waits for them, and re-layouts  1.31 us

commit v1 on v0

--- a/solution.py
+++ b/solution.py
@@ -28,9 +28,9 @@
 def kernel(
     rows, cols, reps, levels, slots, streams,
     rhs_low, rhs_top, inv_low_hbm, inv_top_hbm, blocks_hbm, table_hbm, out_low, out_top,
-    table, table_sem, blocks, inverse, right0, rhs, partial, whole, partial_in, top_in, line, inv_high, inv_rest,
+    table, table_sem, blocks, inverse, right0, rhs, partial, staged, partial_in, top_in, line, inv_high, inv_rest,
     tile_high, tile_rest,
-    load_sem, inv_sem, rhs_sem, right_send, right_recv, part_send, part_recv, top_send, top_recv,
+    load_sem, inv_sem, rhs_sem, right_send, right_recv, half_send, half_recv, part_send, part_recv, top_send, top_recv,
     line_send, line_recv, col_send, col_recv, *columns,
 ):
     row = lax.axis_index("row")
@@ -46,7 +46,7 @@
         pltpu.make_async_copy(blocks_hbm.at[l], blocks.at[l], load_sem.at[l]) for l in range(levels)
     ]
     inv_loads = [
-        pltpu.make_async_copy(inv_low_hbm.at[t] if t < levels else inv_top_hbm, inverse.at[t], inv_sem.at[t])
+        pltpu.make_async_copy(inv_low_hbm.at[t] if t < levels else inv_top_hbm, inverse.at[t, q], inv_sem.at[t])
         for t in range(levels + 1)
     ]
     rhs_loads = [pltpu.make_async_copy(rhs_low.at[0], right0.at[q], rhs_sem.at[0])]
@@ -92,6 +92,18 @@
             device_id=device, device_id_type=MESH,
         )
 
+    def settle():
+        for copy in started:
+            copy.wait_send()
+        started.clear()
+
+        @pl.when(q != b)
+        def _():
+            for copy in conditional:
+                copy.wait_send()
+
+        conditional.clear()
+
     def go(copy):
         copy.start()
         started.append(copy)
@@ -99,14 +111,39 @@
     def begin(d, source, peer):
         return send(rhs_low.at[0], right0.at[source], right_send.at[d], right_recv.at[source], {"col": peer})
 
+    def share_half(t, d, source, peer):
+        return send(
+            inv_low_hbm.at[t] if t < levels else inv_top_hbm, inverse.at[t, source], half_send.at[t, d],
+            half_recv.at[t, source], {"col": peer},
+        )
+
+    def share_inverse(t):
+        for d, peer in enumerate(col_peers):
+            go(share_half(t, d, q, peer))
+
     for d, peer in enumerate(col_peers):
         go(begin(d, q, peer))
+    for t in range(1, levels):
+        share_inverse(t)
 
     def take_inverse(t):
         inv_loads[t].wait()
-        high, low = split(inverse[t])
-        inv_high[t] = high
-        inv_rest[t] = low
+        if t == 0:
+            high, low = split(inverse[t, q])
+            inv_high[t, q] = high
+            inv_rest[t, q] = low
+        else:
+            for d, peer in enumerate(col_peers):
+                share_half(t, d, peer, peer).wait_recv()
+            high, low = split(inverse[t])
+            inv_high[t] = high
+            inv_rest[t] = low
+
+    def apply_inverse(t, s, total):
+        size = cols * part
+        solved = dot3(total, inv_high[t].reshape(size, size), inv_rest[t].reshape(size, size))
+        for j in range(cols):
+            staged[t, s, j] = solved[:, j * part:(j + 1) * part]
 
     def take_rhs(t):
         rhs_loads[t].wait()
@@ -126,20 +163,20 @@
         high_side = share - 1 - jnp.where(i >= mirror, i + 1, i)
         return jnp.where(2 * here < share, low_side, high_side)
 
-    def hop(t, s, source, d, peer, src):
+    def hop(t, s, source, d, target, peer):
         return send(
-            src.at[t, s], partial_in.at[t, source, s], part_send.at[t, d, s], part_recv.at[t, source, s],
+            staged.at[t, s, target], partial_in.at[t, source, s], part_send.at[t, d, s], part_recv.at[t, source, s],
             {"col": peer},
         )
 
-    def exchange(t, s, src):
+    def exchange(t, s):
         for d, peer in enumerate(col_peers):
-            go(hop(t, s, q, d, peer, src))
-
-    def collect(t, s, src):
-        total = src[t, s]
+            go(hop(t, s, q, d, peer, peer))
+
+    def collect(t, s):
+        total = staged[t, s, q]
         for d, peer in enumerate(col_peers):
-            hop(t, s, peer, d, peer, src).wait_recv()
+            hop(t, s, peer, d, peer, peer).wait_recv()
             total = total + partial_in[t, peer, s]
         return total
 
@@ -172,6 +209,7 @@
     residue0 = None
     for l in range(levels):
         pieces = []
+        mark, mark2 = len(started), len(conditional)
         for s in range(streams):
             if l == 0:
                 if s == 0:
@@ -180,14 +218,16 @@
                     rhs_loads[0].wait()
                     residue0 = right0[...].reshape(part * cols, right0.shape[2]).T
                 residue = residue0[s * depth:(s + 1) * depth]
+                solved = dot3(residue, inv_high[0, q], inv_rest[0, q])
             else:
-                residue = collect(l, s, partial)
-            solved = dot3(residue, inv_high[l], inv_rest[l])
+                solved = collect(l, s)
             line[l, s, a] = solved
             for i in reversed(range(share - 1)):
                 go(along(l, s, i, a, order(i, a)))
             spread(l, s, a, share - 1)
             pieces.append(solved)
+        if l == min(1, levels - 1):
+            share_inverse(levels)
         loads[l].wait()
         for k in range(slots):
             high, low = split(blocks[l, k])
@@ -198,6 +238,11 @@
                 c = order(i, a)
                 along(l, s, i, c, c).wait_recv()
                 spread(l, s, c, i)
+        current, waiting = started[mark:], conditional[mark2:]
+        del started[mark:], conditional[mark2:]
+        settle()
+        started.extend(current)
+        conditional.extend(waiting)
         out_low[l] = jnp.concatenate(pieces, axis=0).T
         take_inverse(l + 1)
         if l == 0:
@@ -228,7 +273,8 @@
             later.append((s, products))
             add(l + 1, s, products)
             if l + 1 < levels:
-                exchange(l + 1, s, partial)
+                apply_inverse(l + 1, s, partial[l + 1, s])
+                exchange(l + 1, s)
             if l + 1 == levels:
                 for d, peer in enumerate(rep_peers):
                     go(lift(s, d, peer))
@@ -236,25 +282,24 @@
             for t in range(l + 2, levels + 1):
                 add(t, s, products)
 
+    mark = len(started)
     for s in range(streams):
         total = partial[levels, s]
         for d, peer in enumerate(rep_peers):
             lift(s, d, peer).wait_recv()
             total = total + top_in[d, s]
-        whole[levels, s] = total
-        exchange(levels, s, whole)
+        apply_inverse(levels, s, total)
+        exchange(levels, s)
+    current = started[mark:]
+    del started[mark:]
+    settle()
+    started.extend(current)
     pieces = []
     for s in range(streams):
-        pieces.append(dot3(collect(levels, s, whole), inv_high[levels], inv_rest[levels]))
+        pieces.append(collect(levels, s))
     out_top[...] = jnp.concatenate(pieces, axis=0).T
 
-    for copy in started:
-        copy.wait_send()
-
-    @pl.when(q != b)
-    def _():
-        for copy in conditional:
-            copy.wait_send()
+    settle()
 
 
 def per_device(rows, cols, reps, rhs_low, rhs_top, inv_low, inv_top, blocks, slot_map):
@@ -269,7 +314,7 @@
     share = rows // cols
     vmem = pl.BlockSpec(memory_space=pltpu.VMEM)
     hbm = pl.BlockSpec(memory_space=pltpu.HBM)
-    streams = 4
+    streams = 2
     depth = width // streams
     dma = pltpu.SemaphoreType.DMA
     f32, bf16 = jnp.float32, jnp.bfloat16
@@ -285,16 +330,16 @@
             pltpu.SMEM(table.shape, jnp.int32),
             dma(()),
             pltpu.VMEM((levels, slots, size, size), f32),
-            pltpu.VMEM((levels + 1, part, size), f32),
+            pltpu.VMEM((levels + 1, cols, part, size), f32),
             pltpu.VMEM((cols, part, width), f32),
             pltpu.VMEM((levels + 1, part, width), f32),
             pltpu.VMEM((levels + 1, streams, depth, size), f32),
-            pltpu.VMEM((levels + 1, streams, depth, size), f32),
-            pltpu.VMEM((levels + 1, cols, streams, depth, size), f32),
+            pltpu.VMEM((levels + 1, streams, cols, depth, part), f32),
+            pltpu.VMEM((levels + 1, cols, streams, depth, part), f32),
             pltpu.VMEM((reps - 1, streams, depth, size), f32),
             pltpu.VMEM((levels, streams, share, depth, part), f32),
-            pltpu.VMEM((levels + 1, part, size), bf16),
-            pltpu.VMEM((levels + 1, part, size), bf16),
+            pltpu.VMEM((levels + 1, cols, part, size), bf16),
+            pltpu.VMEM((levels + 1, cols, part, size), bf16),
             pltpu.VMEM((slots, size, size), bf16),
             pltpu.VMEM((slots, size, size), bf16),
             dma((levels,)),
@@ -302,6 +347,8 @@
             dma((levels + 1,)),
             dma((cols - 1,)),
             dma((cols,)),
+            dma((levels + 1, cols - 1)),
+            dma((levels + 1, cols)),
             dma((levels + 1, cols - 1, streams)),
             dma((levels + 1, cols, streams)),
             dma((reps - 1, streams)),

time: 53.2 us -> 52 us (0.977)
  Pallas kernels: 51.1 us -> 49.9 us
    pallas_call x1, Pallas kernels: 51.1 us -> 49.9 us  [per_device(): pl.pallas_call(functools.partial(kernel, rows, cols, reps, levels, slots,...]
where the time goes in v1:
time: 52 us; the launch traced here: 51.8 us
  Pallas kernels  49.9 us (96%)
  local copies, waits for them, and re-layouts  1.31 us (3%)
  between operations  0.64 us (1%)
    pallas_call x1, Pallas kernels, per_device(): pl.pallas_call(functools.partial(kernel, rows, cols, reps, levels, slots,...  49.9 us
    unnamed x2, local copies, waits for them, and re-layouts  1.31 us

profile of v1, /device:TPU:0, one launch (start us, length us, event | category | flops | bytes accessed | tf_op | source)
XLA Modules:
  0.0 51.8 jit_solution(5615846880066853140)
XLA Ops:
  0.6 49.9 %shard_map.77 = (f32[3,128,128]{2,1,0:T(8,128)S(1)}, f32[128,128]{1,0:T(8,128)S(1)}) custom-call(f32[3,128,128]{2,1,0:T(8,128)} %bitcast.16, f32[128,128]{1,0:T(8,128)} %bitcast.18, f32[3,128,256]{2,1,0:T(8,128)} %bitcast.15, f32[128,256]{1,0:T(8,128)} %bitcast.17, f32[3,4,256,256]{3,2,1,0:T(8,128)} %bitcast.14, s32[3,2,4]{2,1,0:T(2,128)} %bitcast.19), custom_call_target="tpu_custom_call" | custom-call | tf_op jit(solution)/shard_map/pallas_call | solution.py:321
  50.5 0.7 %copy.11 = f32[1,3,1,128,128]{4,3,2,1,0:T(8,128)} copy(f32[1,3,1,128,128]{4,3,2,1,0:T(8,128)S(1)} %bitcast.12) | data formatting | bytes 393216
  51.2 0.6 %copy.12 = f32[1,128,128]{2,1,0:T(8,128)} copy(f32[1,128,128]{2,1,0:T(8,128)S(1)} %bitcast.13) | data formatting | bytes 131072
